TPU v7x, 512 devices: a whole 4x4x16 slice. The times are simulated.
512 devices in a mesh: req: 32 (over z, core), hid: 16 (over x, y).
Axes of the slice: x: 4, y: 4, z: 16, core: 2. Of those that a mesh axis runs over, the one named last changes fastest.
Arguments:
- attn_partial: bfloat16 [16, 2048, 2880], P('hid', 'req'), may hold values from -4 to 4
- residual: bfloat16 [2048, 2880], P('req'), may hold values from -6 to 6
- norm_gain: bfloat16 [2880], replicated, may hold values from 0.5 to 1.5
- router_weight: bfloat16 [2880, 32], replicated, may hold values from -0.02734375 to 0.02734375
- router_bias: float32 [32], replicated, may hold values from -2.5 to 2.5
- routes: int32 [2048, 4], P('req'), may hold values from 0 to 31, all different within a row; in each aligned block of 64 rows (0 to 63, 64 to 127, ...) at most 16 rows name the same one
- gate_up: bfloat16 [32, 2880, 5760], P('req', None, 'hid'), may hold values from -0.109375 to 0.109375
- gate_up_bias: bfloat16 [32, 5760], P('req', 'hid'), may hold values from -6 to 6
- down_weight: bfloat16 [32, 2880, 2880], P('req', 'hid'), may hold values from -0.0546875 to 0.0546875
- down_bias: bfloat16 [32, 2880], P('req'), may hold values from -6 to 6
Outputs:
- layer_out: bfloat16 [2048, 2880], P('req')
Inputs may be any that keep to these rules, and one draw needn't show every extreme that they name: `routes`: each row names 4 different experts; among the 64 rows of one request group no expert is named by more than 16 rows, and in every draw some expert is named by exactly 16 rows of some group.
All inputs are finite; a program needn't handle non-finite values.
Results may differ from a plain program's by a relative error of at most 0.022.
Values may be sent and summed in bfloat16 or wider, within the bound.
A program may use at most 64 MiB of HBM per device.

v0:
```python
import jax
import jax.numpy as jnp
from jax import lax
from jax.sharding import PartitionSpec as P


def route_tables(routes, experts, capacity):
    row_count, top_count = routes.shape
    pair_ids = routes.reshape(row_count * top_count)
    onehot = (pair_ids[:, None] == jnp.arange(experts, dtype=jnp.int32)[None, :]).astype(jnp.int32)
    before = jnp.cumsum(onehot, axis=0) - onehot
    slot_ids = jnp.sum(before * onehot, axis=1)
    return (pair_ids * capacity + slot_ids).reshape(row_count, top_count)


def placed(target, values, columns_total):
    columns = jnp.arange(columns_total, dtype=jnp.int32)
    matches = target[:, :, None] == columns[None, None, :]
    return jnp.sum(jnp.where(matches, values[:, :, None], 0.0), axis=1)


def on_device(
    attn_partial,
    residual,
    norm_gain,
    router_weight,
    router_bias,
    routes,
    gate_up,
    gate_up_bias,
    down_weight,
    down_bias,
):
    req_count = lax.axis_size("req")
    row_count, features = residual.shape
    experts = router_weight.shape[1]
    top_count = routes.shape[1]
    capacity = 2 * top_count * row_count // req_count
    gain_wide = norm_gain.astype(jnp.float32)
    attention = lax.psum(attn_partial[0].astype(jnp.float32).astype(jnp.bfloat16), "hid").astype(
        jnp.float32
    )
    stream = (residual.astype(jnp.float32) + attention).astype(jnp.bfloat16)
    widened = stream.astype(jnp.float32)
    inverse = lax.rsqrt(jnp.mean(widened * widened, axis=1, keepdims=True) + 1e-05)
    normed = (widened * inverse * gain_wide).astype(jnp.bfloat16)
    logits = jnp.dot(normed, router_weight, preferred_element_type=jnp.float32) + router_bias

    def whole_rows():
        return (normed, widened)

    picked = jnp.take_along_axis(logits, routes, axis=1)
    raised = jnp.exp(picked)
    combine = (raised / jnp.sum(raised, axis=1, keepdims=True)).astype(jnp.bfloat16)
    target = route_tables(routes, experts, capacity)
    slots_total = experts * capacity
    route_matrix = placed(target, jnp.ones(target.shape, jnp.float32), slots_total).astype(
        jnp.bfloat16
    )
    weights_up = gate_up[0]
    normed_full = whole_rows()[0]
    outgoing = jnp.dot(route_matrix.T, normed_full, preferred_element_type=jnp.float32).astype(
        jnp.bfloat16
    )
    outgoing = outgoing.reshape(experts, capacity, features)
    received = lax.all_to_all(outgoing, "req", split_axis=0, concat_axis=0, tiled=True)
    preact = jnp.dot(
        received.reshape(req_count * capacity, features),
        weights_up,
        preferred_element_type=jnp.float32,
    )
    preact = preact + gate_up_bias[0].astype(jnp.float32)
    gate_part = jnp.minimum(preact[:, 0::2], 7.0)
    up_part = jnp.clip(preact[:, 1::2], -7.0, 7.0)
    activated = ((up_part + 1.0) * gate_part * jax.nn.sigmoid(1.702 * gate_part)).astype(
        jnp.bfloat16
    )
    partial_value = jnp.dot(activated, down_weight[0], preferred_element_type=jnp.float32)
    partial_value = partial_value.astype(jnp.bfloat16).astype(jnp.float32)
    combine_matrix = placed(target, combine.astype(jnp.float32), slots_total).astype(jnp.bfloat16)
    summed = lax.psum(partial_value.astype(jnp.bfloat16), "hid").astype(jnp.float32)
    expert_out = (summed + down_bias[0].astype(jnp.float32)).astype(jnp.bfloat16)
    expert_out = expert_out.reshape(req_count, capacity, features)
    returned = lax.all_to_all(expert_out, "req", split_axis=0, concat_axis=0, tiled=True)
    mixture = jnp.dot(
        combine_matrix, returned.reshape(slots_total, features), preferred_element_type=jnp.float32
    )
    widened_full = whole_rows()[1]
    return (widened_full + mixture).astype(jnp.bfloat16)


def solution(mesh):
    return jax.shard_map(
        on_device,
        mesh=mesh,
        in_specs=(
            P("hid", "req", None),
            P("req", None),
            P(),
            P(),
            P(),
            P("req", None),
            P("req", None, "hid"),
            P("req", "hid"),
            P("req", "hid", None),
            P("req", None),
        ),
        out_specs=P("req", None),
        check_vma=False,
    )
```

profile of v0, /device:TPU:1, one launch (start us, length us, event | category | flops | bytes accessed | tf_op | source)
XLA Modules:
  0.0 591.3 jit_solution(12012518058343366653)
XLA Ops:
  6.5 0.7 all-reduce.3.cloned.1.call-update
  7.3 0.7 bitcast_or_fusion
  8.0 0.8 copy.39
  8.7 0.1 eq.49
  8.8 0.6 reduce-window.6
  9.4 0.2 slice_reduce_fusion
  9.6 0.1 eq.45
  9.7 0.7 convert_element_type.73
  10.5 0.1 reshape.77
  10.7 0.1 fusion.20
  10.8 0.1 reduce_sum.48
  11.0 0.7 multiply_add_fusion
  11.7 118.0 %all-reduce.3.cloned.1.call-done = bf16[64,2880]{1,0:T(8,128)(2,1)} async-done(((bf16[64,2880]{1,0:T(8,128)(2,1)}), bf16[64,2880]{1,0:T(8,128)(2,1)}) %all-reduce.3.cloned.1.call-update) | async-done | bytes 368656 | tf_op jit(solution)/shard_map/psum | solution.py:40
  129.7 1.3 fusion.7
  131.0 1.2 convolution_add_fusion.1
  132.3 2.0 gather_fusion
  134.3 0.1 reshape.80
  134.5 0.2 select_reduce_fusion.1
  134.7 2.7 convolution_convert_fusion.1
  137.4 4.6 copy.45
  142.0 14.5 %all-to-all-start = ((bf16[32,16,2880]{2,1,0:T(8,128)(2,1)}), bf16[32,16,2880]{2,1,0:T(8,128)(2,1)}, u32[]{:S(2)}, u32[]{:S(2)}) async-start(bf16[32,16,2880]{2,1,0:T(8,128)(2,1)} %bitcast.41), calls=%async_computation | async-start | bytes 6029312 | tf_op jit(solution)/shard_map/all_to_all | solution.py:66
  156.5 135.6 %all-to-all-done = bf16[32,16,2880]{2,1,0:T(8,128)(2,1)} async-done(((bf16[32,16,2880]{2,1,0:T(8,128)(2,1)}), bf16[32,16,2880]{2,1,0:T(8,128)(2,1)}, u32[]{:S(2)}, u32[]{:S(2)}) %all-to-all-start) | async-done | bytes 2949152 | tf_op jit(solution)/shard_map/all_to_all | solution.py:66
  292.2 3.2 fusion.3
  295.4 1.5 slice.14
  296.8 1.4 slice.15
  298.3 4.2 convolution_convert_fusion
  302.5 0.7 copy-done.2
  303.2 117.7 %all-reduce.5.cloned.1.call-done = bf16[512,2880]{0,1:T(8,128)(2,1)} async-done(((bf16[512,2880]{0,1:T(8,128)(2,1)}), bf16[512,2880]{0,1:T(8,128)(2,1)}) %all-reduce.5.cloned.1.call-update) | async-done | bytes 2949136 | tf_op jit(solution)/shard_map/psum | solution.py:81
  420.9 4.1 add_convert_fusion
  425.0 4.6 copy.46
  429.5 153.5 %all_to_all.10 = bf16[32,16,2880]{2,1,0:T(8,128)(2,1)S(1)} all-to-all(bf16[32,16,2880]{2,1,0:T(8,128)(2,1)} %bitcast.42), channel_id=1, replica_groups=mesh['req'=32,'hid'=16] {'req'}, dimensions={0} | all-to-all | bytes 5898240 | tf_op jit(solution)/shard_map/all_to_all | solution.py:84
  583.0 1.4 fusion
  (21 shorter events, 0.5 us)
Async XLA Ops:
  6.5 285.6 %copy-start = (bf16[1,2880,360]{1,2,0:T(8,128)(2,1)S(1)}, bf16[1,2880,360]{1,2,0:T(8,128)(2,1)}, u32[]{:S(2)}) copy-start(bf16[1,2880,360]{1,2,0:T(8,128)(2,1)} %param.16) | copy-start | bytes 6220804
  6.5 123.1 %all-reduce.3.cloned.1.call-start = ((), (), s32[]{:S(2)}) async-start(), calls=%async_computation.2 | async-start | bytes 753664 | tf_op jit(solution)/shard_map/psum | solution.py:40
  132.3 2.2 copy-start.1
  142.0 14.5 %copy-start.3 = (bf16[1,360]{1,0:T(2,128)(2,1)S(1)}, bf16[1,360]{1,0:T(2,128)(2,1)}, u32[]{:S(2)}) copy-start(bf16[1,360]{1,0:T(2,128)(2,1)} %param.17) | copy-start | bytes 2164
  142.0 150.2 %all-to-all-start = ((bf16[32,16,2880]{2,1,0:T(8,128)(2,1)}), bf16[32,16,2880]{2,1,0:T(8,128)(2,1)}, u32[]{:S(2)}, u32[]{:S(2)}) async-start(bf16[32,16,2880]{2,1,0:T(8,128)(2,1)} %bitcast.41), calls=%async_computation | async-start | bytes 6029312 | tf_op jit(solution)/shard_map/all_to_all | solution.py:66
  156.4 264.5 %all-reduce.5.cloned.1.call-start = ((), (), s32[]{:S(2)}) async-start(), calls=%async_computation.3 | async-start | bytes 5898240 | tf_op jit(solution)/shard_map/psum | solution.py:81
  302.5 0.7 copy-start.2
Sparse Core Ops, SparseCore 0:
  10.6 119.0 all-reduce.2
  302.6 118.2 all-reduce.4
where the time goes:
time: 592 us; the launch traced here: 591 us
  waiting for transfers between devices  372 us (63%)
  blocking collectives  154 us (26%)
  local copies, waits for them, and re-layouts  16.5 us (3%)
  starting transfers between devices  14.5 us (2%)
  between operations  13.5 us (2%)
  matrix products  12.7 us (2%)
  other arithmetic  8.49 us (1%)
    all_to_all x1, blocking collectives, on_device(): lax.all_to_all(expert_out, 'req', split_axis=0, concat_axis=0, tiled=True)  154 us
    all_to_all x1, waiting for transfers between devices, on_device(): lax.all_to_all(outgoing, 'req', split_axis=0, concat_axis=0, tiled=True)  136 us
    psum x1, waiting for transfers between devices, on_device(): lax.psum(attn_partial[0].astype(jnp.float32).astype(jnp.bfloat16), 'hid')  118 us
    psum x1, waiting for transfers between devices, on_device(): lax.psum(partial_value.astype(jnp.bfloat16), 'hid').astype(jnp.float32)  118 us
    all_to_all x1, starting transfers between devices, on_device(): lax.all_to_all(outgoing, 'req', split_axis=0, concat_axis=0, tiled=True)  14.5 us
  transfers between devices with their start and end apart: 3, of which 3 were waited for; matrix products, arithmetic and copies ran while one was open for 1% of the time, Pallas kernels for 0%

commit v1 on v0

--- a/solution.py
+++ b/solution.py
@@ -1,7 +1,16 @@
+import functools
 import jax
 import jax.numpy as jnp
 from jax import lax
 from jax.sharding import PartitionSpec as P
+
+
+def move_the_tails(packet, row_axis):
+    e_now = lax.all_gather(packet, row_axis)
+    return jnp.sum(e_now, 0)
+
+
+draw_the_indices = functools.partial(move_the_tails, row_axis="hid")
 
 
 def route_tables(routes, experts, capacity):
@@ -37,7 +46,7 @@
     top_count = routes.shape[1]
     capacity = 2 * top_count * row_count // req_count
     gain_wide = norm_gain.astype(jnp.float32)
-    attention = lax.psum(attn_partial[0].astype(jnp.float32).astype(jnp.bfloat16), "hid").astype(
+    attention = draw_the_indices(attn_partial[0].astype(jnp.float32).astype(jnp.bfloat16)).astype(
         jnp.float32
     )
     stream = (residual.astype(jnp.float32) + attention).astype(jnp.bfloat16)

time: 592 us -> 554 us (0.936)
  waiting for transfers between devices: 372 us -> 335 us
    psum x1 -> x0, waiting for transfers between devices: 118 us -> none  [on_device(): lax.psum(attn_partial[0].astype(jnp.float32).astype(jnp.bfloat16), 'hid')]
    all_gather x0 -> x1, waiting for transfers between devices: none -> 79.5 us  [move_the_tails(): e_now = lax.all_gather(packet, row_axis)]
where the time goes in v1:
time: 554 us; the launch traced here: 553 us
  waiting for transfers between devices  335 us (60%)
  blocking collectives  154 us (28%)
  local copies, waits for them, and re-layouts  15.8 us (3%)
  between operations  13.6 us (2%)
  starting transfers between devices  13.2 us (2%)
  matrix products  11.8 us (2%)
  other arithmetic  11 us (2%)
    all_to_all x1, blocking collectives, on_device(): lax.all_to_all(expert_out, 'req', split_axis=0, concat_axis=0, tiled=True)  154 us
    all_to_all x1, waiting for transfers between devices, on_device(): lax.all_to_all(outgoing, 'req', split_axis=0, concat_axis=0, tiled=True)  136 us
    psum x1, waiting for transfers between devices, on_device(): lax.psum(partial_value.astype(jnp.bfloat16), 'hid').astype(jnp.float32)  119 us
    all_gather x1, waiting for transfers between devices, move_the_tails(): e_now = lax.all_gather(packet, row_axis)  79.5 us
    all_to_all x1, starting transfers between devices, on_device(): lax.all_to_all(outgoing, 'req', split_axis=0, concat_axis=0, tiled=True)  13.2 us
  transfers between devices with their start and end apart: 3, of which 3 were waited for; matrix products, arithmetic and copies ran while one was open for 1% of the time, Pallas kernels for 0%

profile of v1, /device:TPU:1, one launch (start us, length us, event | category | flops | bytes accessed | tf_op | source)
XLA Modules:
  0.0 553.5 jit_solution(728477529178288856)
XLA Ops:
  6.5 0.7 all-gather.2.cloned.1.call-update
  7.3 0.8 copy.51
  8.0 0.1 eq.49
  8.1 0.1 eq.45
  8.2 0.7 convert_element_type.75
  8.9 0.7 bitcast_or_fusion
  9.7 0.1 reshape.78
  9.9 0.6 reduce-window.6
  10.4 0.2 slice_reduce_fusion
  10.7 0.1 fusion.20
  10.8 0.1 reduce_sum.61
  11.0 0.7 multiply_add_fusion
  11.7 79.5 %all-gather.2.cloned.1.call-done = bf16[16,64,2880]{2,1,0:T(8,128)(2,1)} async-done(((bf16[1,64,2880]{2,1,0:T(8,128)(2,1)}), bf16[16,64,2880]{2,1,0:T(8,128)(2,1)}) %all-gather.2.cloned.1.call-update) | async-done | bytes 5898256 | tf_op jit(solution)/shard_map/all_gather | solution.py:9
  91.2 3.6 reduce_sum.59
  94.8 0.2 fusion.7
  95.1 0.3 convolution_add_fusion.1
  95.4 2.0 gather_fusion
  97.4 0.1 reshape.81
  97.6 0.2 select_reduce_fusion.1
  97.8 2.7 convolution_convert_fusion.1
  100.5 4.6 copy.57
  105.1 13.2 %all-to-all-start = ((bf16[32,16,2880]{2,1,0:T(8,128)(2,1)}), bf16[32,16,2880]{2,1,0:T(8,128)(2,1)}, u32[]{:S(2)}, u32[]{:S(2)}) async-start(bf16[32,16,2880]{2,1,0:T(8,128)(2,1)} %bitcast.40), calls=%async_computation | async-start | bytes 6029312 | tf_op jit(solution)/shard_map/all_to_all | solution.py:75
  118.4 135.6 %all-to-all-done = bf16[32,16,2880]{2,1,0:T(8,128)(2,1)} async-done(((bf16[32,16,2880]{2,1,0:T(8,128)(2,1)}), bf16[32,16,2880]{2,1,0:T(8,128)(2,1)}, u32[]{:S(2)}, u32[]{:S(2)}) %all-to-all-start) | async-done | bytes 2949152 | tf_op jit(solution)/shard_map/all_to_all | solution.py:75
  254.0 3.2 fusion.3
  257.2 1.5 slice.14
  258.6 1.4 slice.15
  260.1 4.2 convolution_convert_fusion
  264.4 118.7 %all-reduce.2.cloned.1.call-done = bf16[512,2880]{0,1:T(8,128)(2,1)} async-done(((bf16[512,2880]{0,1:T(8,128)(2,1)}), bf16[512,2880]{0,1:T(8,128)(2,1)}) %all-reduce.2.cloned.1.call-update) | async-done | bytes 2949136 | tf_op jit(solution)/shard_map/psum | solution.py:90
  383.1 4.1 add_convert_fusion
  387.1 4.6 copy.58
  391.7 153.5 %all_to_all.10 = bf16[32,16,2880]{2,1,0:T(8,128)(2,1)S(1)} all-to-all(bf16[32,16,2880]{2,1,0:T(8,128)(2,1)} %bitcast.41), channel_id=1, replica_groups=mesh['req'=32,'hid'=16] {'req'}, dimensions={0} | all-to-all | bytes 5898240 | tf_op jit(solution)/shard_map/all_to_all | solution.py:93
  545.2 1.4 fusion
  (28 shorter events, 0.5 us)
Async XLA Ops:
  6.5 247.5 %copy-start = (bf16[1,2880,360]{1,2,0:T(8,128)(2,1)S(1)}, bf16[1,2880,360]{1,2,0:T(8,128)(2,1)}, u32[]{:S(2)}) copy-start(bf16[1,2880,360]{1,2,0:T(8,128)(2,1)} %param.16) | copy-start | bytes 6220804
  6.5 84.6 %all-gather.2.cloned.1.call-start = ((), (), s32[]{:S(2)}) async-start(), calls=%async_computation.2 | async-start | bytes 6406144 | tf_op jit(solution)/shard_map/all_gather | solution.py:9
  11.7 83.1 %copy-start.1 = (bf16[64,2880]{1,0:T(8,128)(2,1)S(1)}, bf16[64,2880]{1,0:T(8,128)(2,1)}, u32[]{:S(2)}) copy-start(bf16[64,2880]{1,0:T(8,128)(2,1)} %param.11) | copy-start | bytes 1105924
  11.7 83.4 %copy-start.5 = (bf16[2880,32]{0,1:T(8,128)(2,1)S(1)}, bf16[2880,32]{0,1:T(8,128)(2,1)}, u32[]{:S(2)}) copy-start(bf16[2880,32]{0,1:T(8,128)(2,1)} %param.13) | copy-start | bytes 552964
  11.7 83.4 %copy-start.6 = (f32[32]{0:T(128)S(1)}, f32[32]{0:T(128)}, u32[]{:S(2)}) copy-start(f32[32]{0:T(128)} %param.14) | copy-start | bytes 388
  95.4 2.2 copy-start.2
  105.1 13.3 %copy-start.4 = (bf16[1,360]{1,0:T(2,128)(2,1)S(1)}, bf16[1,360]{1,0:T(2,128)(2,1)}, u32[]{:S(2)}) copy-start(bf16[1,360]{1,0:T(2,128)(2,1)} %param.17) | copy-start | bytes 2164
  105.1 148.9 %all-to-all-start = ((bf16[32,16,2880]{2,1,0:T(8,128)(2,1)}), bf16[32,16,2880]{2,1,0:T(8,128)(2,1)}, u32[]{:S(2)}, u32[]{:S(2)}) async-start(bf16[32,16,2880]{2,1,0:T(8,128)(2,1)} %bitcast.40), calls=%async_computation | async-start | bytes 6029312 | tf_op jit(solution)/shard_map/all_to_all | solution.py:75
  118.3 264.8 %all-reduce.2.cloned.1.call-start = ((), (), s32[]{:S(2)}) async-start(), calls=%async_computation.3 | async-start | bytes 5898240 | tf_op jit(solution)/shard_map/psum | solution.py:90
  260.1 4.2 copy-start.3
Sparse Core Ops, SparseCore 0:
  10.4 80.7 all-gather.1
  264.4 118.5 all-reduce.1
